TPU v7x, 32 devices: a whole 2x2x4 slice. The times are simulated.
32 devices in a mesh: seq: 8 (over y, x, core), ch: 4 (over z).
Axes of the slice: x: 2, y: 2, z: 4, core: 2. Of those that a mesh axis runs over, the one named last changes fastest.
Arguments:
- inputs: bfloat16 [1536, 131072], P('ch', 'seq'), may hold values from -6 to 6
- gating: bfloat16 [1536, 131072], P('ch', 'seq'), may hold values from -6 to 6
- upstream: bfloat16 [1536, 131072], P('ch', 'seq'), may hold values from -6 to 6
- factor_one: bfloat16 [512, 512], replicated, may hold values from -0.25 to 0.25
- factor_two: bfloat16 [256, 256], replicated, may hold values from -0.375 to 0.375
- factor_three: bfloat16 [256, 256], replicated, may hold values from -0.375 to 0.375
- factor_four: bfloat16 [512, 512], replicated, may hold values from -0.25 to 0.25
- kernel_cols: float32 [1536, 512], P('ch'), may hold values from -4 to 4
- kernel_rows: float32 [1536, 256], P('ch'), may hold values from -4 to 4
Outputs:
- input_grad: bfloat16 [1536, 131072], P('ch', 'seq')
- gating_grad: bfloat16 [1536, 131072], P('ch', 'seq')
- one_grad: float32 [512, 512], replicated
- two_grad: float32 [256, 256], replicated
- three_grad: float32 [256, 256], replicated
- four_grad: float32 [512, 512], replicated
- cols_grad: float32 [1536, 512], P('ch')
- rows_grad: float32 [1536, 256], P('ch')
All inputs are finite; a program needn't handle non-finite values.
Results may differ from a plain program's by a relative error of at most 0.0076.
Values may be sent and summed in bfloat16 or wider, within the bound.
A program may use at most 384 MiB of HBM per device.

v0:
```python
import math
import jax
import jax.numpy as jnp
from jax import lax
from jax.sharding import PartitionSpec as P

P1 = 256
P2 = 512
C = 1536


def local(
    inputs,
    gating,
    upstream,
    factor_one,
    factor_two,
    factor_three,
    factor_four,
    kernel_cols,
    kernel_rows,
):
    width = inputs.shape[0]
    length = inputs.shape[1]
    parts = lax.axis_size("seq")
    flt = jnp.float32
    half = jnp.bfloat16
    rows_local = length // P2
    up_gate = (upstream.astype(flt) * gating.astype(flt)).astype(half)
    moved_in, moved_gate = (
        lax.all_to_all(inputs, "seq", split_axis=0, concat_axis=1, tiled=True),
        lax.all_to_all(up_gate, "seq", split_axis=0, concat_axis=1, tiled=True),
    )
    several = width // parts
    offset = lax.axis_index("seq") * several
    local_cols = lax.dynamic_slice_in_dim(kernel_cols, offset, several, 0)
    local_rows = lax.dynamic_slice_in_dim(kernel_rows, offset, several, 0)
    shaped = moved_in.reshape(several, P1, P2)
    gate_rows = moved_gate.reshape(several, P1, P2)
    first_prod = jnp.einsum("cij,jk->cik", shaped, factor_one, preferred_element_type=flt)
    first_out = (first_prod * local_cols[:, None, :]).astype(half)
    left_prod = jnp.einsum("ki,cij->ckj", factor_two, first_out, preferred_element_type=flt)
    left_out = (left_prod * local_rows[:, :, None]).astype(half)
    second = jnp.einsum("ki,cij->ckj", factor_three, left_out, preferred_element_type=flt).astype(
        half
    )
    grad_four = jnp.einsum("cij,cik->jk", second, gate_rows, preferred_element_type=flt)
    grad_second = jnp.einsum(
        "cik,jk->cij", gate_rows, factor_four, preferred_element_type=flt
    ).astype(half)
    grad_three = jnp.einsum("ckj,cij->ki", grad_second, left_out, preferred_element_type=flt)
    grad_left = jnp.einsum("ki,ckj->cij", factor_three, grad_second, preferred_element_type=flt)
    rows_part = jnp.sum(grad_left * left_prod, axis=2)
    grad_prod = (grad_left * local_rows[:, :, None]).astype(half)
    grad_two = jnp.einsum("ckj,cij->ki", grad_prod, first_out, preferred_element_type=flt)
    grad_first = jnp.einsum(
        "ki,ckj->cij", factor_two, grad_prod, preferred_element_type=flt
    ).astype(half)
    cols_part = jnp.sum(grad_first.astype(flt) * first_prod, axis=1)
    grad_inner = (grad_first.astype(flt) * local_cols[:, None, :]).astype(half)
    grad_one = jnp.einsum("cij,cik->jk", shaped, grad_inner, preferred_element_type=flt)
    local_input = jnp.einsum(
        "cik,jk->cij", grad_inner, factor_one, preferred_element_type=flt
    ).astype(half)
    input_grad, second_rows = (
        lax.all_to_all(
            local_input.reshape(several, P1 * P2), "seq", split_axis=1, concat_axis=0, tiled=True
        ),
        lax.all_to_all(
            second.reshape(several, P1 * P2), "seq", split_axis=1, concat_axis=0, tiled=True
        ),
    )
    cols_sum, rows_sum = (
        lax.all_gather(cols_part, "seq", axis=0, tiled=True),
        lax.all_gather(rows_part, "seq", axis=0, tiled=True),
    )
    final_prod = jnp.einsum(
        "cij,jk->cik",
        second_rows.reshape(width, rows_local, P2),
        factor_four,
        preferred_element_type=flt,
    )
    gating_grad = (
        (upstream.reshape(width, rows_local, P2).astype(flt) * final_prod)
        .astype(half)
        .reshape(width, length)
    )
    one_sum, two_sum, three_sum, four_sum = lax.psum(
        (grad_one, grad_two, grad_three, grad_four), ("seq", "ch")
    )
    scale_one = 1.0 / math.sqrt(P1 * C)
    scale_two = 1.0 / math.sqrt(P2 * C)
    return (
        input_grad,
        gating_grad,
        one_sum * scale_one,
        two_sum * scale_two,
        three_sum * scale_two,
        four_sum * scale_one,
        cols_sum / math.sqrt(P1),
        rows_sum / math.sqrt(P2),
    )


def solution(mesh):
    in_specs = (
        P("ch", "seq"),
        P("ch", "seq"),
        P("ch", "seq"),
        P(),
        P(),
        P(),
        P(),
        P("ch", None),
        P("ch", None),
    )
    out_specs = (P("ch", "seq"), P("ch", "seq"), P(), P(), P(), P(), P("ch", None), P("ch", None))
    return jax.shard_map(local, mesh=mesh, in_specs=in_specs, out_specs=out_specs, check_vma=False)
```

profile of v0, /device:TPU:0, one launch (start us, length us, event | category | flops | bytes accessed | tf_op | source)
XLA Modules:
  0.0 879.9 jit_solution(3477879930901490185)
XLA Ops:
  17.1 144.0 %all_to_all.67 = bf16[8,48,16384]{2,1,0:T(8,128)(2,1)} all-to-all(bf16[8,48,16384]{2,1,0:T(8,128)(2,1)S(1)} %bitcast.84), channel_id=1, replica_groups=mesh['seq'=8,'ch'=4] {'seq'}, dimensions={0} | all-to-all | bytes 25165824 | tf_op jit(solution)/shard_map/all_to_all | solution.py:32
  167.3 14.4 %copy.71 = bf16[48,8,16384]{2,1,0:T(8,128)(2,1)} copy(bf16[48,8,16384]{2,0,1:T(8,128)(2,1)} %bitcast.82) | data formatting | bytes 25165824 | tf_op jit(solution)/shard_map/all_to_all | solution.py:32
  181.7 19.5 %reshape.52 = bf16[48,256,512]{2,1,0:T(8,128)(2,1)} reshape(bf16[48,8,16384]{2,1,0:T(8,128)(2,1)} %copy.71) | data formatting | bytes 25165824 | tf_op jit(solution)/shard_map/reshape | solution.py:39
  227.5 14.8 %convolution_convert_fusion = bf16[48,512,256]{1,2,0:T(8,128)(2,1)} fusion(f32[48,512,256]{2,1,0:T(8,128)} %fusion.39, f32[48,256]{1,0:T(8,128)S(1)} %constant_dynamic-slice_fusion.1, bf16[256,256]{1,0:T(8,128)(2,1)S(1)} %copy-done.6), kind=kOutput, calls=%fused_computation.17 | convolution fusion | flops 3240099840 | bytes 37928960 | tf_op jit(solution)/shard_map/ki,ckj->cij/dot_general | solution.py:56
  256.7 19.8 %all_to_all.53 = bf16[48,8,16384]{2,1,0:T(8,128)(2,1)} reshape(bf16[48,256,512]{2,1,0:T(8,128)(2,1)} %fusion.10) | data formatting | bytes 25165824 | tf_op jit(solution)/shard_map/all_to_all | solution.py:66
  276.5 14.5 %copy.75 = bf16[48,8,16384]{2,0,1:T(8,128)(2,1)} copy(bf16[48,8,16384]{2,1,0:T(8,128)(2,1)} %all_to_all.53) | data formatting | bytes 25165824 | tf_op jit(solution)/shard_map/all_to_all | solution.py:66
  291.0 14.5 %all-to-all-done.2 = bf16[8,48,16384]{2,1,0:T(8,128)(2,1)} async-done(((bf16[8,48,16384]{2,1,0:T(8,128)(2,1)}), bf16[8,48,16384]{2,1,0:T(8,128)(2,1)}, u32[]{:S(2)}, u32[]{:S(2)}) %all-to-all-start.2) | async-done | bytes 12582944 | tf_op jit(solution)/shard_map/all_to_all | solution.py:31
  310.8 17.6 %copy.76 = f32[384,16384]{0,1:T(8,128)} copy(bf16[384,16384]{1,0:T(8,128)(2,1)} %param.11) | data formatting | bytes 37748736 | tf_op jit(solution)/shard_map/convert_element_type | solution.py:29
  328.4 24.6 %copy.82 = f32[384,32,512]{2,0,1:T(8,128)} copy(f32[384,32,512]{0,2,1:T(8,128)} %bitcast.80) | data formatting | bytes 50331648 | tf_op jit(solution)/shard_map/convert_element_type | solution.py:84
  367.4 19.5 %reshape.53 = bf16[48,256,512]{2,1,0:T(8,128)(2,1)} reshape(bf16[48,8,16384]{2,1,0:T(8,128)(2,1)} %copy.77) | data formatting | bytes 25165824 | tf_op jit(solution)/shard_map/reshape | solution.py:38
  387.0 18.9 %fusion.1 = (f32[48,512]{1,0:T(8,128)}, f32[48,256,512]{2,1,0:T(8,128)}) fusion(bf16[48,512,256]{1,2,0:T(8,128)(2,1)} %convolution_convert_fusion, bf16[48,256,512]{2,1,0:T(8,128)(2,1)} %reshape.53, bf16[512,512]{1,0:T(8,128)(2,1)S(1)} %copy-done.3), kind=kOutput, calls=%fused_computation.3 | convolution fusion | flops 6461300736 | bytes 50954240 | tf_op jit(solution)/shard_map/cij,jk->cik/dot_general | solution.py:40
  405.9 16.3 %fusion.21 = f32[48,512,256]{2,1,0:T(8,128)} fusion(f32[48,256,512]{2,1,0:T(8,128)} %get-tuple-element.45, f32[48,512]{1,0:T(8,128)S(1)} %constant_dynamic-slice_fusion, bf16[256,256]{1,0:T(8,128)(2,1)S(1)} %copy-done.6), kind=kOutput, calls=%fused_computation.22 | convolution fusion | flops 3233808384 | bytes 50561024 | tf_op jit(solution)/shard_map/ki,cij->ckj/dot_general | solution.py:42
  422.2 14.5 %convert_bitcast_fusion = bf16[48,256,512]{1,2,0:T(8,128)(2,1)} fusion(f32[48,512,256]{2,1,0:T(8,128)} %fusion.21, f32[48,256]{1,0:T(8,128)S(1)} %constant_dynamic-slice_fusion.1, bf16[256,256]{1,0:T(8,128)(2,1)S(1)} %copy-done.7), kind=kOutput, calls=%fused_computation.14 | convolution fusion | flops 3240099840 | bytes 37928960 | tf_op jit(solution)/shard_map/ki,cij->ckj/dot_general | solution.py:44
  436.7 16.7 %copy.79 = bf16[48,256,512]{2,1,0:T(8,128)(2,1)} copy(bf16[48,256,512]{1,2,0:T(8,128)(2,1)} %convert_bitcast_fusion) | data formatting | bytes 25165824 | tf_op jit(solution)/shard_map/convert_element_type | solution.py:44
  453.4 19.5 %all_to_all.60 = bf16[48,8,16384]{2,1,0:T(8,128)(2,1)} reshape(bf16[48,256,512]{2,1,0:T(8,128)(2,1)} %copy.79) | data formatting | bytes 25165824 | tf_op jit(solution)/shard_map/all_to_all | solution.py:69
  472.9 26.0 %copy.80 = bf16[48,8,16384]{2,0,1:T(8,128)(2,1)} copy(bf16[48,8,16384]{2,1,0:T(8,128)(2,1)} %all_to_all.60) | data formatting | bytes 25165824 | tf_op jit(solution)/shard_map/all_to_all | solution.py:69
  499.0 16.0 %fusion.28 = f32[256,256]{1,0:T(8,128)} fusion(bf16[48,256,512]{2,1,0:T(8,128)(2,1)} %copy-done.2, f32[48,512,256]{2,1,0:T(8,128)} %fusion.21, f32[48,256]{1,0:T(8,128)S(1)} %constant_dynamic-slice_fusion.1), kind=kOutput, calls=%fused_computation.26 | convolution fusion | flops 3233808384 | bytes 38060032 | tf_op jit(solution)/shard_map/ckj,cij->ki/dot_general | solution.py:51
  547.0 17.6 %fusion.25 = f32[256,256]{1,0:T(8,128)} fusion(f32[48,256,512]{2,1,0:T(8,128)} %get-tuple-element.45, f32[48,512]{1,0:T(8,128)S(1)} %constant_dynamic-slice_fusion, f32[48,512,256]{2,1,0:T(8,128)} %fusion.39, f32[48,256]{1,0:T(8,128)S(1)} %constant_dynamic-slice_fusion.1), kind=kOutput, calls=%fused_computation.25 | convolution fusion | flops 3246391296 | bytes 50741248 | tf_op jit(solution)/shard_map/ckj,cij->ki/dot_general | solution.py:55
  564.6 16.7 %multiply_reduce_fusion = f32[48,256]{1,0:T(8,128)S(1)} fusion(f32[48,512,256]{2,1,0:T(8,128)} %fusion.39, f32[48,512,256]{2,1,0:T(8,128)} %fusion.21), kind=kLoop, calls=%fused_computation.4 | loop fusion | flops 12570624 | bytes 50380800 | tf_op jit(solution)/shard_map/reduce_sum | solution.py:53
  581.3 89.7 %all_gather.7 = f32[384,256]{1,0:T(8,128)S(1)} all-gather(f32[48,256]{1,0:T(8,128)S(1)} %multiply_reduce_fusion), channel_id=1, replica_groups=mesh['seq'=8,'ch'=4] {'seq'}, dimensions={0}, use_global_device_ids=true | all-gather | bytes 442368 | tf_op jit(solution)/shard_map/all_gather | solution.py:75
  682.0 62.6 %all-reduce.3.cloned.1.call-done = (f32[512,512]{0,1:T(8,128)}, f32[256,256]{1,0:T(8,128)}, f32[256,256]{1,0:T(8,128)}, f32[512,512]{0,1:T(8,128)}) async-done(((f32[512,512]{0,1:T(8,128)}, f32[256,256]{1,0:T(8,128)}, f32[256,256]{1,0:T(8,128)}, f32[512,512]{0,1:T(8,128)}), (f32[512,512]{0,1:T(8,128)}, f32[256,256]{1,0:T(8,128)}, f32[256,256]{1,0:T(8,128)}, ...) | async-done | bytes 2621456 | tf_op jit(solution)/shard_map/psum | solution.py:88
  763.6 65.3 %multiply_convert_fusion = bf16[384,32,512]{2,0,1:T(8,128)(2,1)} fusion(f32[384,32,512]{2,0,1:T(8,128)} %copy.82, bf16[384,32,512]{2,1,0:T(8,128)(2,1)} %bitcast.81, bf16[512,512]{1,0:T(8,128)(2,1)S(1)} %copy-done.5), kind=kOutput, calls=%fused_computation.5 | convolution fusion | flops 6455033856 | bytes 50855936 | tf_op jit(solution)/shard_map/cij,jk->cik/dot_general | solution.py:77
  828.9 16.7 %copy.83 = bf16[384,32,512]{0,2,1:T(8,128)(2,1)} copy(bf16[384,32,512]{2,0,1:T(8,128)(2,1)} %multiply_convert_fusion) | data formatting | bytes 25165824 | tf_op jit(solution)/shard_map/convert_element_type | solution.py:85
  845.6 16.6 %copy.88 = bf16[384,16384]{1,0:T(8,128)(2,1)} copy(bf16[384,16384]{0,1:T(8,128)(2,1)} %bitcast.83) | data formatting | bytes 25165824
  (43 shorter events, 149.1 us)
Async XLA Ops:
  7.2 160.1 %copy-start = (f32[384,512]{1,0:T(8,128)S(1)}, f32[384,512]{1,0:T(8,128)}, u32[]{:S(2)}) copy-start(f32[384,512]{1,0:T(8,128)} %param.16) | copy-start | bytes 2359300
  161.1 144.4 %all-to-all-start.2 = ((bf16[8,48,16384]{2,1,0:T(8,128)(2,1)}), bf16[8,48,16384]{2,1,0:T(8,128)(2,1)}, u32[]{:S(2)}, u32[]{:S(2)}) async-start(bf16[8,48,16384]{2,1,0:T(8,128)(2,1)} %bitcast.85), calls=%async_computation.2 | async-start | bytes 25165824 | tf_op jit(solution)/shard_map/all_to_all | solution.py:31
  181.7 19.5 %copy-start.4 = (bf16[512,512]{1,0:T(8,128)(2,1)S(1)}, bf16[512,512]{1,0:T(8,128)(2,1)}, u32[]{:S(2)}) copy-start(bf16[512,512]{1,0:T(8,128)(2,1)} %param.15) | copy-start | bytes 1572868
  201.3 16.1 %copy-start.7 = (bf16[256,256]{1,0:T(8,128)(2,1)S(1)}, bf16[256,256]{1,0:T(8,128)(2,1)}, u32[]{:S(2)}) copy-start(bf16[256,256]{1,0:T(8,128)(2,1)} %param.14) | copy-start | bytes 393220
  212.8 4.5 copy-start.2
  217.4 10.1 %copy-start.6 = (bf16[256,256]{1,0:T(8,128)(2,1)S(1)}, bf16[256,256]{1,0:T(8,128)(2,1)}, u32[]{:S(2)}) copy-start(bf16[256,256]{1,0:T(8,128)(2,1)} %param.13) | copy-start | bytes 393220
  227.5 14.8 %copy-start.3 = (bf16[512,512]{1,0:T(8,128)(2,1)S(1)}, bf16[512,512]{1,0:T(8,128)(2,1)}, u32[]{:S(2)}) copy-start(bf16[512,512]{1,0:T(8,128)(2,1)} %param.12) | copy-start | bytes 1572868
  305.4 209.5 %all-to-all-start.1 = ((bf16[48,8,16384]{2,0,1:T(8,128)(2,1)}), bf16[48,8,16384]{2,0,1:T(8,128)(2,1)}, u32[]{:S(2)}, u32[]{:S(2)}) async-start(bf16[48,8,16384]{2,0,1:T(8,128)(2,1)} %copy.75), calls=%async_computation.1 | async-start | bytes 25165824 | tf_op jit(solution)/shard_map/all_to_all | solution.py:66
  514.9 235.9 %all-to-all-start.3 = ((bf16[48,8,16384]{2,0,1:T(8,128)(2,1)}), bf16[48,8,16384]{2,0,1:T(8,128)(2,1)}, u32[]{:S(2)}, u32[]{:S(2)}) async-start(bf16[48,8,16384]{2,0,1:T(8,128)(2,1)} %copy.80), calls=%async_computation.3 | async-start | bytes 25165824 | tf_op jit(solution)/shard_map/all_to_all | solution.py:69
  520.3 224.3 %all-reduce.3.cloned.1.call-start = ((), (), s32[]{:S(2)}) async-start(), calls=%async_computation.4 | async-start | bytes 5242880 | tf_op jit(solution)/shard_map/psum | solution.py:88
  564.6 106.4 %copy-start.8 = (f32[48,512]{1,0:T(8,128)S(1)}, f32[48,512]{1,0:T(8,128)}, u32[]{:S(2)}) copy-start(f32[48,512]{1,0:T(8,128)} %get-tuple-element.44) | copy-start | bytes 294916
  750.8 12.8 %copy-start.5 = (bf16[512,512]{1,0:T(8,128)(2,1)S(1)}, bf16[512,512]{1,0:T(8,128)(2,1)}, u32[]{:S(2)}) copy-start(bf16[512,512]{1,0:T(8,128)(2,1)} %param.15) | copy-start | bytes 1572868
  862.2 10.5 %copy-start.1 = (f32[384,512]{1,0:T(8,128)S(1)}, f32[384,512]{1,0:T(8,128)}, u32[]{:S(2)}) copy-start(f32[384,512]{1,0:T(8,128)} %param.16) | copy-start | bytes 2359300
Sparse Core Ops, SparseCore 0:
  564.7 179.7 all-reduce.2
where the time goes:
time: 894 us; the launch traced here: 880 us
  local copies, waits for them, and re-layouts  271 us (30%)
  blocking collectives  243 us (27%)
  matrix products  226 us (25%)
  waiting for transfers between devices  77.1 us (9%)
  other arithmetic  31.9 us (4%)
  starting transfers between devices  16.1 us (2%)
  between operations  14.5 us (2%)
    all_to_all x1, blocking collectives, local(): lax.all_to_all(up_gate, 'seq', split_axis=0, concat_axis=1, tiled=True)  144 us
    all_gather x1, blocking collectives, local(): lax.all_gather(rows_part, 'seq', axis=0, tiled=True)  89.7 us
    dot_general x1, matrix products, local(): jnp.einsum('cij,jk->cik', second_rows.reshape(width, rows_local, P2), fac...  65.3 us
    psum x1, waiting for transfers between devices, local(): lax.psum((grad_one, grad_two, grad_three, grad_four), ('seq', 'ch'))  62.6 us
    unnamed x23, local copies, waits for them, and re-layouts  47.1 us
    all_to_all x2, local copies, waits for them, and re-layouts, local(): lax.all_to_all(second.reshape(several, P1 * P2), 'seq', split_axis=1, con...  45.5 us
    all_to_all x2, local copies, waits for them, and re-layouts, local(): lax.all_to_all(local_input.reshape(several, P1 * P2), 'seq', split_axis=1...  34.3 us
    convert_element_type x1, local copies, waits for them, and re-layouts, local(): upstream.reshape(width, rows_local, P2).astype(flt) * final_prod  24.6 us
  transfers between devices with their start and end apart: 4, of which 2 were waited for; matrix products, arithmetic and copies ran while one was open for 40% of the time, Pallas kernels for 0%

commit v1 on v0

--- a/solution.py
+++ b/solution.py
@@ -7,6 +7,30 @@
 P1 = 256
 P2 = 512
 C = 1536
+
+
+def split_up(array, dim, devices):
+    shape = array.shape
+    tiles = array.reshape(*shape[:dim], devices, shape[dim] // devices, *shape[dim + 1 :])
+    return jnp.moveaxis(tiles, dim, 0)
+
+
+def laid_out(blocks, dim):
+    blocks = jnp.moveaxis(blocks, 0, dim)
+    shape = blocks.shape
+    return blocks.reshape(*shape[:dim], shape[dim] * shape[dim + 1], *shape[dim + 2 :])
+
+
+def exchange_directly(value, axis, split_dim, concat_dim):
+    peers, index = (lax.axis_size(axis), lax.axis_index(axis))
+    blocks = split_up(value, split_dim, peers)
+    whole = blocks
+    for step in range(1, peers):
+        target, source = ((index + step) % peers, (index - step) % peers)
+        sent = lax.dynamic_index_in_dim(blocks, target, 0)
+        received = lax.ppermute(sent, axis, [(i, (i + step) % peers) for i in range(peers)])
+        whole = lax.dynamic_update_slice_in_dim(whole, received, source, axis=0)
+    return laid_out(whole, concat_dim)
 
 
 def local(
@@ -29,7 +53,7 @@
     up_gate = (upstream.astype(flt) * gating.astype(flt)).astype(half)
     moved_in, moved_gate = (
         lax.all_to_all(inputs, "seq", split_axis=0, concat_axis=1, tiled=True),
-        lax.all_to_all(up_gate, "seq", split_axis=0, concat_axis=1, tiled=True),
+        exchange_directly(up_gate, "seq", 0, 1),
     )
     several = width // parts
     offset = lax.axis_index("seq") * several

time: 894 us -> 1030 us (1.15)
  waiting for transfers between devices: 77.1 us -> 323 us
  blocking collectives: 243 us -> 99 us
  starting transfers between devices: 16.1 us -> 45.2 us
  local copies, waits for them, and re-layouts: 271 us -> 282 us
    ppermute x0 -> x7, waiting for transfers between devices: none -> 260 us  [exchange_directly(): lax.ppermute(sent, axis, [(i, (i + step) % peers) for i in range(peers)])]
    all_to_all x1 -> x0, blocking collectives: 144 us -> none  [local(): lax.all_to_all(up_gate, 'seq', split_axis=0, concat_axis=1, tiled=True)]
    all_to_all x1, starting transfers between devices: 5.33 us -> 27.9 us  [local(): lax.all_to_all(local_input.reshape(several, P1 * P2), 'seq', split_axis=1...]
    reshape x1 -> x0, local copies, waits for them, and re-layouts: 19.5 us -> none  [local(): gate_rows = moved_gate.reshape(several, P1, P2)]
    another operation x0 -> x1, local copies, waits for them, and re-layouts: none -> 19.5 us  [local(): gate_rows = moved_gate.reshape(several, P1, P2)]
    transpose x0 -> x1, local copies, waits for them, and re-layouts: none -> 14.6 us  [laid_out(): blocks = jnp.moveaxis(blocks, 0, dim)]
    all_to_all x1, waiting for transfers between devices: 14.5 us -> 0.01 us  [local(): lax.all_to_all(inputs, 'seq', split_axis=0, concat_axis=1, tiled=True)]
    all_to_all x1 -> x0, local copies, waits for them, and re-layouts: 14.4 us -> none  [local(): lax.all_to_all(up_gate, 'seq', split_axis=0, concat_axis=1, tiled=True)]
  transfers between devices with their start and end apart: 4 -> 11, of which waited for: 2 -> 4; matrix products, arithmetic and copies ran while one was open for 40% -> 34% of each run, Pallas kernels for 0% -> 0%
where the time goes in v1:
time: 1030 us; the launch traced here: 1020 us
  waiting for transfers between devices  323 us (31%)
  local copies, waits for them, and re-layouts  282 us (27%)
  matrix products  226 us (22%)
  blocking collectives  99 us (10%)
  starting transfers between devices  45.2 us (4%)
  other arithmetic  31.9 us (3%)
  between operations  14.7 us (1%)
    ppermute x7, waiting for transfers between devices, exchange_directly(): lax.ppermute(sent, axis, [(i, (i + step) % peers) for i in range(peers)])  260 us
    all_gather x1, blocking collectives, local(): lax.all_gather(rows_part, 'seq', axis=0, tiled=True)  89.8 us
    dot_general x1, matrix products, local(): jnp.einsum('cij,jk->cik', second_rows.reshape(width, rows_local, P2), fac...  65.3 us
    psum x1, waiting for transfers between devices, local(): lax.psum((grad_one, grad_two, grad_three, grad_four), ('seq', 'ch'))  62.7 us
    unnamed x25, local copies, waits for them, and re-layouts  51.9 us
    all_to_all x2, local copies, waits for them, and re-layouts, local(): lax.all_to_all(local_input.reshape(several, P1 * P2), 'seq', split_axis=1...  34.5 us
    all_to_all x2, local copies, waits for them, and re-layouts, local(): lax.all_to_all(second.reshape(several, P1 * P2), 'seq', split_axis=1, con...  34.2 us
    all_to_all x1, starting transfers between devices, local(): lax.all_to_all(local_input.reshape(several, P1 * P2), 'seq', split_axis=1...  27.9 us
  transfers between devices with their start and end apart: 11, of which 4 were waited for; matrix products, arithmetic and copies ran while one was open for 34% of the time, Pallas kernels for 0%

profile of v1, /device:TPU:0, one launch (start us, length us, event | category | flops | bytes accessed | tf_op | source)
XLA Modules:
  0.0 1021.3 jit_solution(3204902498421775959)
XLA Ops:
  22.5 21.1 %collective-permute-done = bf16[1,48,16384]{2,1,0:T(8,128)(2,1)} collective-permute-done((bf16[1,48,16384]{2,1,0:T(8,128)(2,1)S(1)}, bf16[1,48,16384]{2,1,0:T(8,128)(2,1)}, u32[]{:S(2)}, u32[]{:S(2)}) %collective-permute-start) | collective-permute-done | bytes 1572896 | tf_op jit(solution)/shard_map/ppermute | solution.py:31
  63.8 26.2 %collective-permute-done.1 = bf16[1,48,16384]{2,1,0:T(8,128)(2,1)} collective-permute-done((bf16[1,48,16384]{2,1,0:T(8,128)(2,1)}, bf16[1,48,16384]{2,1,0:T(8,128)(2,1)}, u32[]{:S(2)}, u32[]{:S(2)}) %collective-permute-start.1) | collective-permute-done | bytes 1572896 | tf_op jit(solution)/shard_map/ppermute | solution.py:31
  92.7 212.5 %collective-permute-done.2 = bf16[1,48,16384]{2,1,0:T(8,128)(2,1)S(1)} collective-permute-done((bf16[1,48,16384]{2,1,0:T(8,128)(2,1)}, bf16[1,48,16384]{2,1,0:T(8,128)(2,1)S(1)}, u32[]{:S(2)}, u32[]{:S(2)}) %collective-permute-start.2) | collective-permute-done | bytes 1572896 | tf_op jit(solution)/shard_map/ppermute | solution.py:31
  311.5 14.6 %copy.90 = bf16[48,8,16384]{2,1,0:T(8,128)(2,1)} copy(bf16[48,8,16384]{2,0,1:T(8,128)(2,1)} %bitcast.82) | data formatting | bytes 25165824 | tf_op jit(solution)/shard_map/transpose | solution.py:19
  326.1 19.5 %reshape_reshape.3 = bf16[48,256,512]{2,1,0:T(8,128)(2,1)} reshape(bf16[48,8,16384]{2,1,0:T(8,128)(2,1)} %copy.90) | data formatting | bytes 25165824 | tf_op jit(solution)/shard_map/reshape;reshape | solution.py:63
  371.9 14.8 %convolution_convert_fusion = bf16[48,512,256]{1,2,0:T(8,128)(2,1)} fusion(f32[48,512,256]{2,1,0:T(8,128)} %fusion.39, f32[48,256]{1,0:T(8,128)S(1)} %constant_dynamic-slice_fusion.1, bf16[256,256]{1,0:T(8,128)(2,1)S(1)} %copy-done.7), kind=kOutput, calls=%fused_computation.17 | convolution fusion | flops 3240099840 | bytes 37928960 | tf_op jit(solution)/shard_map/ki,ckj->cij/dot_general | solution.py:80
  401.0 20.0 %all_to_all.38 = bf16[48,8,16384]{2,1,0:T(8,128)(2,1)} reshape(bf16[48,256,512]{2,1,0:T(8,128)(2,1)} %fusion.10) | data formatting | bytes 25165824 | tf_op jit(solution)/shard_map/all_to_all | solution.py:90
  435.5 27.9 %all-to-all-start = ((bf16[48,8,16384]{2,0,1:T(8,128)(2,1)}), bf16[48,8,16384]{2,0,1:T(8,128)(2,1)}, u32[]{:S(2)}, u32[]{:S(2)}) async-start(bf16[48,8,16384]{2,0,1:T(8,128)(2,1)} %copy.94), calls=%async_computation | async-start | bytes 25165824 | tf_op jit(solution)/shard_map/all_to_all | solution.py:90
  463.4 17.6 %copy.95 = f32[384,16384]{0,1:T(8,128)} copy(bf16[384,16384]{1,0:T(8,128)(2,1)} %param.11) | data formatting | bytes 37748736 | tf_op jit(solution)/shard_map/convert_element_type | solution.py:53
  481.0 24.7 %copy.101 = f32[384,32,512]{2,0,1:T(8,128)} copy(f32[384,32,512]{0,2,1:T(8,128)} %bitcast.83) | data formatting | bytes 50331648 | tf_op jit(solution)/shard_map/convert_element_type | solution.py:108
  520.1 19.6 %reshape.49 = bf16[48,256,512]{2,1,0:T(8,128)(2,1)} reshape(bf16[48,8,16384]{2,1,0:T(8,128)(2,1)} %copy.96) | data formatting | bytes 25165824 | tf_op jit(solution)/shard_map/reshape | solution.py:62
  539.7 18.9 %fusion.1 = (f32[48,512]{1,0:T(8,128)}, f32[48,256,512]{2,1,0:T(8,128)}) fusion(bf16[48,512,256]{1,2,0:T(8,128)(2,1)} %convolution_convert_fusion, bf16[48,256,512]{2,1,0:T(8,128)(2,1)} %reshape.49, bf16[512,512]{1,0:T(8,128)(2,1)S(1)} %copy-done.4), kind=kOutput, calls=%fused_computation.3 | convolution fusion | flops 6461300736 | bytes 50954240 | tf_op jit(solution)/shard_map/cij,jk->cik/dot_general | solution.py:64
  558.6 16.3 %fusion.21 = f32[48,512,256]{2,1,0:T(8,128)} fusion(f32[48,256,512]{2,1,0:T(8,128)} %get-tuple-element.60, f32[48,512]{1,0:T(8,128)S(1)} %constant_dynamic-slice_fusion, bf16[256,256]{1,0:T(8,128)(2,1)S(1)} %copy-done.7), kind=kOutput, calls=%fused_computation.22 | convolution fusion | flops 3233808384 | bytes 50561024 | tf_op jit(solution)/shard_map/ki,cij->ckj/dot_general | solution.py:66
  589.3 16.7 %copy.98 = bf16[48,256,512]{2,1,0:T(8,128)(2,1)} copy(bf16[48,256,512]{1,2,0:T(8,128)(2,1)} %convert_bitcast_fusion) | data formatting | bytes 25165824 | tf_op jit(solution)/shard_map/convert_element_type | solution.py:68
  605.9 19.6 %all_to_all.45 = bf16[48,8,16384]{2,1,0:T(8,128)(2,1)} reshape(bf16[48,256,512]{2,1,0:T(8,128)(2,1)} %copy.98) | data formatting | bytes 25165824 | tf_op jit(solution)/shard_map/all_to_all | solution.py:93
  625.5 14.6 %copy.99 = bf16[48,8,16384]{2,0,1:T(8,128)(2,1)} copy(bf16[48,8,16384]{2,1,0:T(8,128)(2,1)} %all_to_all.45) | data formatting | bytes 25165824 | tf_op jit(solution)/shard_map/all_to_all | solution.py:93
  640.1 15.9 %fusion.28 = f32[256,256]{1,0:T(8,128)} fusion(bf16[48,256,512]{2,1,0:T(8,128)(2,1)} %copy-done.2, f32[48,512,256]{2,1,0:T(8,128)} %fusion.21, f32[48,256]{1,0:T(8,128)S(1)} %constant_dynamic-slice_fusion.1), kind=kOutput, calls=%fused_computation.26 | convolution fusion | flops 3233808384 | bytes 38060032 | tf_op jit(solution)/shard_map/ckj,cij->ki/dot_general | solution.py:75
  688.2 17.6 %fusion.25 = f32[256,256]{1,0:T(8,128)} fusion(f32[48,256,512]{2,1,0:T(8,128)} %get-tuple-element.60, f32[48,512]{1,0:T(8,128)S(1)} %constant_dynamic-slice_fusion, f32[48,512,256]{2,1,0:T(8,128)} %fusion.39, f32[48,256]{1,0:T(8,128)S(1)} %constant_dynamic-slice_fusion.1), kind=kOutput, calls=%fused_computation.25 | convolution fusion | flops 3246391296 | bytes 50741248 | tf_op jit(solution)/shard_map/ckj,cij->ki/dot_general | solution.py:79
  705.8 16.6 %multiply_reduce_fusion = f32[48,256]{1,0:T(8,128)S(1)} fusion(f32[48,512,256]{2,1,0:T(8,128)} %fusion.39, f32[48,512,256]{2,1,0:T(8,128)} %fusion.21), kind=kLoop, calls=%fused_computation.4 | loop fusion | flops 12570624 | bytes 50380800 | tf_op jit(solution)/shard_map/reduce_sum | solution.py:77
  722.5 89.8 %all_gather.7 = f32[384,256]{1,0:T(8,128)S(1)} all-gather(f32[48,256]{1,0:T(8,128)S(1)} %multiply_reduce_fusion), channel_id=1, replica_groups=mesh['seq'=8,'ch'=4] {'seq'}, dimensions={0}, use_global_device_ids=true | all-gather | bytes 442368 | tf_op jit(solution)/shard_map/all_gather | solution.py:99
  823.2 62.7 %all-reduce.3.cloned.1.call-done = (f32[512,512]{0,1:T(8,128)}, f32[256,256]{1,0:T(8,128)}, f32[256,256]{1,0:T(8,128)}, f32[512,512]{0,1:T(8,128)}) async-done(((f32[512,512]{0,1:T(8,128)}, f32[256,256]{1,0:T(8,128)}, f32[256,256]{1,0:T(8,128)}, f32[512,512]{0,1:T(8,128)}), (f32[512,512]{0,1:T(8,128)}, f32[256,256]{1,0:T(8,128)}, f32[256,256]{1,0:T(8,128)}, ...) | async-done | bytes 2621456 | tf_op jit(solution)/shard_map/psum | solution.py:112
  905.0 65.3 %multiply_convert_fusion = bf16[384,32,512]{2,0,1:T(8,128)(2,1)} fusion(f32[384,32,512]{2,0,1:T(8,128)} %copy.101, bf16[384,32,512]{2,1,0:T(8,128)(2,1)} %bitcast.84, bf16[512,512]{1,0:T(8,128)(2,1)S(1)} %copy-done.6), kind=kOutput, calls=%fused_computation.5 | convolution fusion | flops 6455033856 | bytes 50855936 | tf_op jit(solution)/shard_map/cij,jk->cik/dot_general | solution.py:101
  970.3 16.6 %copy.102 = bf16[384,32,512]{0,2,1:T(8,128)(2,1)} copy(bf16[384,32,512]{2,0,1:T(8,128)(2,1)} %multiply_convert_fusion) | data formatting | bytes 25165824 | tf_op jit(solution)/shard_map/convert_element_type | solution.py:109
  986.9 16.6 %copy.107 = bf16[384,16384]{1,0:T(8,128)(2,1)} copy(bf16[384,16384]{0,1:T(8,128)(2,1)} %bitcast.85) | data formatting | bytes 25165824
  (66 shorter events, 200.9 us)
Async XLA Ops:
  7.2 52.0 %copy-start = (f32[384,512]{1,0:T(8,128)S(1)}, f32[384,512]{1,0:T(8,128)}, u32[]{:S(2)}) copy-start(f32[384,512]{1,0:T(8,128)} %param.16) | copy-start | bytes 2359300
  17.1 4.8 copy-start.3
  22.0 21.6 %collective-permute-start = (bf16[1,48,16384]{2,1,0:T(8,128)(2,1)S(1)}, bf16[1,48,16384]{2,1,0:T(8,128)(2,1)}, u32[]{:S(2)}, u32[]{:S(2)}) collective-permute-start(bf16[1,48,16384]{2,1,0:T(8,128)(2,1)S(1)} %constant_dynamic-slice_fusion.8), channel_id=1, source_target_pairs={{0,4},{4,8},{8,12},{12,16},{16,20},{20,24},{24,28},{28,0},{1,5},{5... | collective-permute-start | bytes 4718600 | tf_op jit(solution)/shard_map/ppermute | solution.py:31
  51.5 38.5 %collective-permute-start.1 = (bf16[1,48,16384]{2,1,0:T(8,128)(2,1)}, bf16[1,48,16384]{2,1,0:T(8,128)(2,1)}, u32[]{:S(2)}, u32[]{:S(2)}) collective-permute-start(bf16[1,48,16384]{2,1,0:T(8,128)(2,1)} %get-tuple-element.57), channel_id=1, source_target_pairs={{0,8},{4,12},{8,16},{12,20},{16,24},{20,28},{24,0},{28,4},{1,9},{5... | collective-permute-start | bytes 4718600 | tf_op jit(solution)/shard_map/ppermute | solution.py:31
  52.9 382.7 %all-to-all-start.1 = ((bf16[8,48,16384]{2,1,0:T(8,128)(2,1)}), bf16[8,48,16384]{2,1,0:T(8,128)(2,1)}, u32[]{:S(2)}, u32[]{:S(2)}) async-start(bf16[8,48,16384]{2,1,0:T(8,128)(2,1)} %bitcast.86), calls=%async_computation.1 | async-start | bytes 25165824 | tf_op jit(solution)/shard_map/all_to_all | solution.py:55
  59.2 251.0 %collective-permute-start.6 = (bf16[1,48,16384]{2,1,0:T(8,128)(2,1)S(1)}, bf16[1,48,16384]{2,1,0:T(8,128)(2,1)S(1)}, u32[]{:S(2)}, u32[]{:S(2)}) collective-permute-start(bf16[1,48,16384]{2,1,0:T(8,128)(2,1)S(1)} %get-tuple-element.52), channel_id=1, source_target_pairs={{0,28},{4,0},{8,4},{12,8},{16,12},{20,16},{24,20},{28,24},{1,29},{... | collective-permute-start | bytes 4718600 | tf_op jit(solution)/shard_map/ppermute | solution.py:31
  61.7 247.3 %collective-permute-start.5 = (bf16[1,48,16384]{2,1,0:T(8,128)(2,1)}, bf16[1,48,16384]{2,1,0:T(8,128)(2,1)S(1)}, u32[]{:S(2)}, u32[]{:S(2)}) collective-permute-start(bf16[1,48,16384]{2,1,0:T(8,128)(2,1)} %get-tuple-element.53), channel_id=1, source_target_pairs={{0,24},{4,28},{8,0},{12,4},{16,8},{20,12},{24,16},{28,20},{1,25},{... | collective-permute-start | bytes 4718600 | tf_op jit(solution)/shard_map/ppermute | solution.py:31
  62.2 245.5 %collective-permute-start.4 = (bf16[1,48,16384]{2,1,0:T(8,128)(2,1)}, bf16[1,48,16384]{2,1,0:T(8,128)(2,1)S(1)}, u32[]{:S(2)}, u32[]{:S(2)}) collective-permute-start(bf16[1,48,16384]{2,1,0:T(8,128)(2,1)} %get-tuple-element.54), channel_id=1, source_target_pairs={{0,20},{4,24},{8,28},{12,0},{16,4},{20,8},{24,12},{28,16},{1,21},{... | collective-permute-start | bytes 4718600 | tf_op jit(solution)/shard_map/ppermute | solution.py:31
  63.0 243.5 %collective-permute-start.3 = (bf16[1,48,16384]{2,1,0:T(8,128)(2,1)}, bf16[1,48,16384]{2,1,0:T(8,128)(2,1)S(1)}, u32[]{:S(2)}, u32[]{:S(2)}) collective-permute-start(bf16[1,48,16384]{2,1,0:T(8,128)(2,1)} %get-tuple-element.55), channel_id=1, source_target_pairs={{0,16},{4,20},{8,24},{12,28},{16,0},{20,4},{24,8},{28,12},{1,17},{... | collective-permute-start | bytes 4718600 | tf_op jit(solution)/shard_map/ppermute | solution.py:31
  90.0 215.2 %collective-permute-start.2 = (bf16[1,48,16384]{2,1,0:T(8,128)(2,1)}, bf16[1,48,16384]{2,1,0:T(8,128)(2,1)S(1)}, u32[]{:S(2)}, u32[]{:S(2)}) collective-permute-start(bf16[1,48,16384]{2,1,0:T(8,128)(2,1)} %get-tuple-element.56), channel_id=1, source_target_pairs={{0,12},{4,16},{8,20},{12,24},{16,28},{20,0},{24,4},{28,8},{1,13},{... | collective-permute-start | bytes 4718600 | tf_op jit(solution)/shard_map/ppermute | solution.py:31
  326.1 19.5 %copy-start.5 = (bf16[512,512]{1,0:T(8,128)(2,1)S(1)}, bf16[512,512]{1,0:T(8,128)(2,1)}, u32[]{:S(2)}) copy-start(bf16[512,512]{1,0:T(8,128)(2,1)} %param.15) | copy-start | bytes 1572868
  345.6 16.2 %copy-start.8 = (bf16[256,256]{1,0:T(8,128)(2,1)S(1)}, bf16[256,256]{1,0:T(8,128)(2,1)}, u32[]{:S(2)}) copy-start(bf16[256,256]{1,0:T(8,128)(2,1)} %param.14) | copy-start | bytes 393220
  357.2 4.6 copy-start.2
  361.8 10.1 copy-start.7
  371.9 14.8 %copy-start.4 = (bf16[512,512]{1,0:T(8,128)(2,1)S(1)}, bf16[512,512]{1,0:T(8,128)(2,1)}, u32[]{:S(2)}) copy-start(bf16[512,512]{1,0:T(8,128)(2,1)} %param.12) | copy-start | bytes 1572868
  435.5 220.6 %all-to-all-start = ((bf16[48,8,16384]{2,0,1:T(8,128)(2,1)}), bf16[48,8,16384]{2,0,1:T(8,128)(2,1)}, u32[]{:S(2)}, u32[]{:S(2)}) async-start(bf16[48,8,16384]{2,0,1:T(8,128)(2,1)} %copy.94), calls=%async_computation | async-start | bytes 25165824 | tf_op jit(solution)/shard_map/all_to_all | solution.py:90
  656.1 236.1 %all-to-all-start.2 = ((bf16[48,8,16384]{2,0,1:T(8,128)(2,1)}), bf16[48,8,16384]{2,0,1:T(8,128)(2,1)}, u32[]{:S(2)}, u32[]{:S(2)}) async-start(bf16[48,8,16384]{2,0,1:T(8,128)(2,1)} %copy.99), calls=%async_computation.2 | async-start | bytes 25165824 | tf_op jit(solution)/shard_map/all_to_all | solution.py:93
  661.4 224.5 %all-reduce.3.cloned.1.call-start = ((), (), s32[]{:S(2)}) async-start(), calls=%async_computation.3 | async-start | bytes 5242880 | tf_op jit(solution)/shard_map/psum | solution.py:112
  705.8 106.4 %copy-start.9 = (f32[48,512]{1,0:T(8,128)S(1)}, f32[48,512]{1,0:T(8,128)}, u32[]{:S(2)}) copy-start(f32[48,512]{1,0:T(8,128)} %get-tuple-element.59) | copy-start | bytes 294916
  892.2 12.8 %copy-start.6 = (bf16[512,512]{1,0:T(8,128)(2,1)S(1)}, bf16[512,512]{1,0:T(8,128)(2,1)}, u32[]{:S(2)}) copy-start(bf16[512,512]{1,0:T(8,128)(2,1)} %param.15) | copy-start | bytes 1572868
  1003.5 10.5 %copy-start.1 = (f32[384,512]{1,0:T(8,128)S(1)}, f32[384,512]{1,0:T(8,128)}, u32[]{:S(2)}) copy-start(f32[384,512]{1,0:T(8,128)} %param.16) | copy-start | bytes 2359300
Sparse Core Ops, SparseCore 0:
  705.9 179.9 all-reduce.2
